TPU v7x, 32 devices: a whole 2x2x4 slice. The times are simulated.
32 devices in a mesh: groups: 2 (over x), tr: 16 (over z, y, core).
Axes of the slice: x: 2, y: 2, z: 4, core: 2. Of those that a mesh axis runs over, the one named last changes fastest.
Arguments:
- object_field: float32 [2, 16384, 1024], P(None, ('groups', 'tr')), parts along dimension 1, may hold values from -6 to 6
- probe_modes: float32 [2, 2, 256, 256], replicated, may hold values from -96 to 96
- scan_offsets: int32 [32, 8, 2], P(('groups', 'tr')), parts along dimension 0, may hold values from 0 to 768, as said below
- scan_counts: int32 [32], P(('groups', 'tr')), parts along dimension 0, may hold values from 1 to 8, as said below
- measured: int32 [32, 8, 256, 256], P(('groups', 'tr')), parts along dimension 0, may hold values from 0 to 4096
Outputs:
- object_grad: float32 [2, 16384, 1024], P(None, ('groups', 'tr')), parts along dimension 1
- probe_grad: float32 [2048, 256], P(('groups', 'tr')), parts along dimension 0
There are 2 independent parts, one for each index of `groups`. A program takes and returns all parts, laid end to end along the dimension named above; an argument that names none is the same for every part. Nothing has to cross between parts.
Inputs may be any that keep to these rules, and one draw needn't show every extreme that they name: `scan_counts`: each tile has 1 to 8 used scan positions, and some tile has exactly 8. `scan_offsets`: row offsets lie in 0 to 511 within the tile, column offsets in 0 to 768; both ends are reached; every slot holds a valid offset, used or not.
All inputs are finite; a program needn't handle non-finite values.
Results may differ from a plain program's by a relative error of at most 0.0095.
Values may be sent and summed in bfloat16 or wider, within the bound.
No kernel may reach another device: no remote copies, remote signals or barrier semaphores. Data moves between devices by JAX's collectives and lax.ppermute only.
A program may use at most 64 MiB of HBM per device.

v0:
```python
import jax
import jax.numpy as jnp
from jax import lax
from jax.sharding import PartitionSpec as P

loss_scale = 1.0 / 1024.0


def shifted(value, axis, steps):
    count = lax.axis_size(axis)
    initial, last = (max(0, -steps), min(count, count - steps))
    return lax.ppermute(value, axis, [(source, source + steps) for source in range(initial, last)])


def dft_table(patch_size):
    index_run = jnp.arange(patch_size, dtype=jnp.int32)
    product = index_run[:, None] * index_run[None, :] % patch_size
    phase_angle = -2.0 * jnp.pi / patch_size * product.astype(jnp.float32)
    unit_scale = 1.0 / jnp.sqrt(jnp.float32(patch_size))
    table_real = jnp.cos(phase_angle) * unit_scale
    table_imag = jnp.sin(phase_angle) * unit_scale
    upper_rows = jnp.concatenate([table_real, table_imag], axis=1)
    lower_rows = jnp.concatenate([-table_imag, table_real], axis=1)
    return jnp.concatenate([upper_rows, lower_rows], axis=0).astype(jnp.bfloat16)


def forward_part(patch, sqrt_counts, probe_modes, dft_matrix):
    patch_size = patch.shape[-1]
    mode_count = probe_modes.shape[0]
    probe_real = probe_modes[:, 0]
    probe_imag = probe_modes[:, 1]
    object_real = patch[0]
    object_imag = patch[1]
    exit_real = probe_real * object_real - probe_imag * object_imag
    exit_imag = probe_real * object_imag + probe_imag * object_real
    exit_wave = jnp.concatenate([exit_real, exit_imag], axis=-1).astype(jnp.bfloat16)
    half_done = jnp.einsum(
        "mpk,kl->mpl", exit_wave, dft_matrix, preferred_element_type=jnp.float32
    ).astype(jnp.bfloat16)
    stacked = jnp.concatenate([half_done[..., :patch_size], half_done[..., patch_size:]], axis=1)
    far_field = jnp.einsum("kq,mkp->mqp", dft_matrix, stacked, preferred_element_type=jnp.float32)
    far_real = far_field[:, :patch_size]
    far_imag = far_field[:, patch_size:]
    model_power = jnp.sum(far_real * far_real + far_imag * far_imag, axis=0)
    factor = 2.0 * loss_scale * (1.0 - sqrt_counts / jnp.sqrt(model_power + 1.0))
    return (
        (far_field.reshape(mode_count, 2, patch_size, patch_size) * factor)
        .reshape(mode_count, 2 * patch_size, patch_size)
        .astype(jnp.bfloat16)
    )


def backward_part(grad_far, patch, probe_modes, dft_matrix):
    patch_size = patch.shape[-1]
    probe_real = probe_modes[:, 0]
    probe_imag = probe_modes[:, 1]
    object_real = patch[0]
    object_imag = patch[1]
    back_rows = jnp.einsum(
        "qk,mkp->mqp", dft_matrix, grad_far, preferred_element_type=jnp.float32
    ).astype(jnp.bfloat16)
    col_major = jnp.concatenate([back_rows[:, :patch_size], back_rows[:, patch_size:]], axis=-1)
    grad_wave = jnp.einsum("mpk,lk->mpl", col_major, dft_matrix, preferred_element_type=jnp.float32)
    grad_real = grad_wave[..., :patch_size]
    grad_imag = grad_wave[..., patch_size:]
    obj_real = jnp.sum(probe_real * grad_real + probe_imag * grad_imag, axis=0)
    obj_imag = jnp.sum(probe_real * grad_imag - probe_imag * grad_real, axis=0)
    probe_greal = object_real * grad_real + object_imag * grad_imag
    probe_gimag = object_real * grad_imag - object_imag * grad_real
    return (jnp.stack([obj_real, obj_imag]), jnp.stack([probe_greal, probe_gimag], axis=1))


def patch_grads(patch, sqrt_counts, probe_modes, dft_matrix):
    grad_far = forward_part(patch, sqrt_counts, probe_modes, dft_matrix)
    return backward_part(grad_far, patch, probe_modes, dft_matrix)


def add_block(gradient, block, offset_pair):
    corner = (jnp.int32(0), offset_pair[0], offset_pair[1])
    current = lax.dynamic_slice(gradient, corner, block.shape)
    return lax.dynamic_update_slice(gradient, current + block, corner)


def on_device(object_field, probe_modes, scan_offsets, scan_counts, measured):
    patch_size = probe_modes.shape[-1]
    strip_rows = object_field.shape[1]
    dft_matrix = dft_table(patch_size)
    lower_band = shifted(object_field[:, :patch_size, :], "tr", -1)
    extended = jnp.concatenate([object_field, lower_band], axis=1)
    sqrt_counts = jnp.sqrt(measured[0].astype(jnp.float32))
    offsets = scan_offsets[0]
    own_count = scan_counts[0]

    def extract_patch(offset_pair):
        return lax.dynamic_slice(
            extended, (jnp.int32(0), offset_pair[0], offset_pair[1]), (2, patch_size, patch_size)
        )

    def local_slot(slot_index, loop_state):
        gradient, probe_sum = loop_state
        offset_pair = offsets[slot_index]
        part_object, part_probe = patch_grads(
            extract_patch(offset_pair), sqrt_counts[slot_index], probe_modes, dft_matrix
        )
        return (add_block(gradient, part_object, offset_pair), probe_sum + part_probe)

    zero_grad = jnp.zeros(extended.shape, jnp.float32)
    zero_probe = jnp.zeros(probe_modes.shape, jnp.float32)
    gradient, probe_sum = lax.fori_loop(
        jnp.int32(0), own_count, local_slot, (zero_grad, zero_probe)
    )
    edge_grad = shifted(gradient[:, strip_rows:, :], "tr", 1)
    object_grad = gradient[:, :strip_rows, :] + jnp.pad(
        edge_grad, ((0, 0), (0, strip_rows - patch_size), (0, 0))
    )
    flat_probe = probe_sum.reshape(-1, patch_size)
    whole_probe = lax.psum(flat_probe, "tr")
    share_rows = flat_probe.shape[0] // lax.axis_size("tr")
    probe_grad = lax.dynamic_slice_in_dim(
        whole_probe, lax.axis_index("tr") * share_rows, share_rows, 0
    )
    return (object_grad, probe_grad)


def solution(mesh):
    return jax.shard_map(
        on_device,
        mesh=mesh,
        in_specs=(
            P(None, ("groups", "tr"), None),
            P(),
            P(("groups", "tr"), None, None),
            P(("groups", "tr")),
            P(("groups", "tr"), None, None, None),
        ),
        out_specs=(P(None, ("groups", "tr"), None), P(("groups", "tr"), None)),
        check_vma=False,
    )
```

profile of v0, /device:TPU:0, one launch (start us, length us, event | category | flops | bytes accessed | tf_op | source)
XLA Modules:
  0.0 312.3 jit_solution(7520786833410476199)
XLA Ops:
  7.2 0.0 copy-start.1
  7.2 0.0 all-reduce.3.cloned.1.call-start
  7.2 3.2 %slice.59 = f32[2,256,1024]{2,1,0:T(8,128)} slice(f32[2,512,1024]{2,1,0:T(8,128)} %param.7), slice={[0:2], [0:256], [0:1024]} | slice | bytes 4194304 | tf_op jit(solution)/shard_map/slice | solution.py:88
  10.5 1.3 collective-permute-start
  11.7 0.0 copy-done.1
  11.8 0.1 copy.10
  11.8 2.9 copy.9
  14.8 0.0 copy-start
  14.8 1.0 fusion.37
  15.8 1.1 negate_convert_fusion
  16.9 3.5 %sqrt_bitcast_fusion = f32[8,256,256]{1,2,0:T(8,128)} fusion(s32[1,8,256,256]{2,3,1,0:T(8,128)} %copy.9), kind=kLoop, calls=%fused_computation.55 | loop fusion | flops 524288 | bytes 4194304 | tf_op jit(solution)/shard_map/sqrt | solution.py:90
  20.4 0.0 collective-permute-done
  20.4 0.0 copy-done
  20.4 5.1 %pad_maximum_fusion = f32[2,768,1024]{2,1,0:T(8,128)} fusion(f32[2,256,1024]{2,1,0:T(8,128)} %collective-permute-done, f32[2,512,1024]{2,1,0:T(8,128)S(1)} %copy-done), kind=kLoop, calls=%fused_computation.53 | loop fusion | flops 1572864 | bytes 12582912 | tf_op jit(solution)/shard_map/concatenate | solution.py:89
  25.5 0.0 copy-start.2
  25.5 0.1 broadcast_in_dim.10
  25.6 3.4 %broadcast_in_dim.4 = f32[2,768,1024]{2,1,0:T(8,128)} broadcast(f32[]{:T(128)} %constant.22.clone.1), dimensions={} | broadcast | bytes 6291460 | tf_op jit(solution)/shard_map/broadcast_in_dim | solution.py:107
  29.0 0.0 copy-done.2
  29.0 19.2 %while.12 = (s32[]{:T(128)}, f32[2,768,1024]{2,1,0:T(8,128)}, f32[2,2,256,256]{3,2,0,1:T(8,128)S(1)}, s32[]{:T(128)}, s32[8,2]{0,1:T(2,128)S(1)}, /*index=5*/f32...) while((s32[]{:T(128)}, f32[2,768,1024]{2,1,0:T(8,128)}, ...), condition=%wide.region_4.5_spmd, body=%wide.region_0.4_spmd.sunk | while | flops 1082195968 | bytes 27525448 | solution.py:109
  29.7 0.1 constant_dynamic-slice_fusion.3
  29.8 0.6 fusion.63
  34.1 1.3 dynamic-slice_bitcast_fusion.3
  35.5 0.2 fusion.64
  35.6 0.4 convolution_convert_fusion.3
  36.1 0.5 convolution_bitcast_fusion.2
  36.6 0.1 fusion.66
  36.7 1.0 fusion.67
  37.7 0.2 mul.321
  37.9 0.5 fusion.68
  38.4 0.5 fusion.70
  38.9 0.3 add_bitcast_fusion.2
  39.2 1.4 maximum_add_fusion.4
  40.6 0.3 maximum_add_fusion.5
  40.8 6.7 %dynamic_update_slice.4 = f32[2,768,1024]{2,1,0:T(8,128)} dynamic-update-slice(f32[2,768,1024]{2,1,0:T(8,128)} %get-tuple-element.198, f32[2,256,256]{2,1,0:T(8,128)S(1)} %maximum_add_fusion.4, s32[]{:T(128)} %constant.12.clone.1..sunk, s32[]{:T(128)S(6)} %select_n.47, s32[]{:T(128)S(6)} %select_n.48) | dynamic-update-slice | bytes 1048580 | tf_op jit(solution)/shard_map/while/body/dynamic_update_slice | solution.py:81
  48.2 3.2 %slice.61 = f32[2,256,1024]{2,1,0:T(8,128)} slice(f32[2,768,1024]{2,1,0:T(8,128)} %get-tuple-element.51), slice={[0:2], [512:768], [0:1024]} | slice | bytes 4194304 | tf_op jit(solution)/shard_map/slice | solution.py:112
  51.4 151.8 %collective-permute-start.1 = (f32[2,256,1024]{2,1,0:T(8,128)}, f32[2,256,1024]{2,1,0:T(8,128)}, u32[]{:S(2)}, u32[]{:S(2)}) collective-permute-start(f32[2,256,1024]{2,1,0:T(8,128)} %slice.61), channel_id=1, source_target_pairs={{0,1},{1,2},{2,3},{3,4},{4,5},{5,6},{6,7},{7,8},{8,9},{9,10},{10,1... | collective-permute-start | bytes 6291464 | tf_op jit(solution)/shard_map/ppermute | solution.py:12
  203.2 1.0 copy.11
  204.2 0.0 all-reduce.3.cloned.1.call-update
  204.2 94.0 %all-reduce.3.cloned.1.call-done = f32[1024,256]{1,0:T(8,128)} async-done(((f32[1024,256]{1,0:T(8,128)}), f32[1024,256]{1,0:T(8,128)}) %all-reduce.3.cloned.1.call-update) | async-done | bytes 1048592 | tf_op jit(solution)/shard_map/psum | solution.py:117
  298.2 1.5 constant_dynamic-slice_fusion.1
  299.7 0.0 collective-permute-done.1
  299.7 5.8 %pad_add_fusion = f32[2,512,1024]{2,1,0:T(8,128)} fusion(f32[2,256,1024]{2,1,0:T(8,128)} %collective-permute-done.1, f32[2,768,1024]{2,1,0:T(8,128)} %get-tuple-element.51), kind=kLoop, calls=%fused_computation.54 | loop fusion | flops 1048576 | bytes 10485760 | tf_op jit(solution)/shard_map/add | solution.py:113
  (4 shorter events, 0.1 us)
Async XLA Ops:
  7.2 4.6 %copy-start.1 = (f32[2,2,256,256]{3,2,1,0:T(8,128)S(1)}, f32[2,2,256,256]{3,2,1,0:T(8,128)}, u32[]{:S(2)}) copy-start(f32[2,2,256,256]{3,2,1,0:T(8,128)} %param.8) | copy-start | bytes 3145732
  7.2 291.0 %all-reduce.3.cloned.1.call-start = ((), (), s32[]{:S(2)}) async-start(), calls=%async_computation | async-start | bytes 2097152 | tf_op jit(solution)/shard_map/psum | solution.py:117
  10.5 9.9 %collective-permute-start = (f32[2,256,1024]{2,1,0:T(8,128)}, f32[2,256,1024]{2,1,0:T(8,128)}, u32[]{:S(2)}, u32[]{:S(2)}) collective-permute-start(f32[2,256,1024]{2,1,0:T(8,128)} %slice.59), channel_id=1, source_target_pairs={{1,0},{2,1},{3,2},{4,3},{5,4},{6,5},{7,6},{8,7},{9,8},{10,9},{11,1... | collective-permute-start | bytes 6291464 | tf_op jit(solution)/shard_map/ppermute | solution.py:12
  14.8 5.6 %copy-start = (f32[2,512,1024]{2,1,0:T(8,128)S(1)}, f32[2,512,1024]{2,1,0:T(8,128)}, u32[]{:S(2)}) copy-start(f32[2,512,1024]{2,1,0:T(8,128)} %param.7) | copy-start | bytes 12582916
  25.5 3.5 %copy-start.2 = (s32[1,8,2]{1,2,0:T(2,128)S(1)}, s32[1,8,2]{1,2,0:T(2,128)}, u32[]{:S(2)}) copy-start(s32[1,8,2]{1,2,0:T(2,128)} %param.9) | copy-start | bytes 196
  51.4 248.3 %collective-permute-start.1 = (f32[2,256,1024]{2,1,0:T(8,128)}, f32[2,256,1024]{2,1,0:T(8,128)}, u32[]{:S(2)}, u32[]{:S(2)}) collective-permute-start(f32[2,256,1024]{2,1,0:T(8,128)} %slice.61), channel_id=1, source_target_pairs={{0,1},{1,2},{2,3},{3,4},{4,5},{5,6},{6,7},{7,8},{8,9},{9,10},{10,1... | collective-permute-start | bytes 6291464 | tf_op jit(solution)/shard_map/ppermute | solution.py:12
Sparse Core Ops, SparseCore 0:
  204.4 93.8 all-reduce.2
where the time goes:
time: 315 us; the launch traced here: 312 us
  starting transfers between devices  153 us (49%)
  waiting for transfers between devices  94 us (30%)
  local copies, waits for them, and re-layouts  24.5 us (8%)
  other arithmetic  19.6 us (6%)
  between operations  14.1 us (4%)
  loops' own time  5.21 us (2%)
    ppermute x2, starting transfers between devices, shifted(): lax.ppermute(value, axis, [(source, source + steps) for source in range(i...  153 us
    psum x1, waiting for transfers between devices, on_device(): whole_probe = lax.psum(flat_probe, 'tr')  94 us
    dynamic_update_slice x1, local copies, waits for them, and re-layouts, add_block(): return lax.dynamic_update_slice(gradient, current + block, corner)  6.72 us
  transfers between devices with their start and end apart: 3, of which 1 were waited for; matrix products, arithmetic and copies ran while one was open for 4% of the time, Pallas kernels for 0%

commit v1 on v0

--- a/solution.py
+++ b/solution.py
@@ -114,7 +114,7 @@
         edge_grad, ((0, 0), (0, strip_rows - patch_size), (0, 0))
     )
     flat_probe = probe_sum.reshape(-1, patch_size)
-    whole_probe = lax.psum(flat_probe, "tr")
+    whole_probe = jnp.sum(lax.all_gather(flat_probe, "tr"), axis=0)
     share_rows = flat_probe.shape[0] // lax.axis_size("tr")
     probe_grad = lax.dynamic_slice_in_dim(
         whole_probe, lax.axis_index("tr") * share_rows, share_rows, 0

time: 315 us -> 353 us (1.12)
  waiting for transfers between devices: 94 us -> 125 us
  other arithmetic: 19.6 us -> 26.4 us
    all_gather x0 -> x1, waiting for transfers between devices: none -> 121 us  [on_device(): whole_probe = jnp.sum(lax.all_gather(flat_probe, 'tr'), axis=0)]
    psum x1 -> x0, waiting for transfers between devices: 94 us -> none  [on_device(): whole_probe = lax.psum(flat_probe, 'tr')]
    reduce_sum x0 -> x1, other arithmetic: none -> 6.98 us  [on_device(): whole_probe = jnp.sum(lax.all_gather(flat_probe, 'tr'), axis=0)]
    ppermute x2, waiting for transfers between devices: 0.01 us -> 3.84 us  [shifted(): lax.ppermute(value, axis, [(source, source + steps) for source in range(i...]
  transfers between devices with their start and end apart: 3 -> 3, of which waited for: 1 -> 2; matrix products, arithmetic and copies ran while one was open for 4% -> 5% of each run, Pallas kernels for 0% -> 0%
where the time goes in v1:
time: 353 us; the launch traced here: 350 us
  starting transfers between devices  153 us (43%)
  waiting for transfers between devices  125 us (35%)
  other arithmetic  26.4 us (7%)
  local copies, waits for them, and re-layouts  23.7 us (7%)
  between operations  14.1 us (4%)
  loops' own time  5.42 us (2%)
    ppermute x2, starting transfers between devices, shifted(): lax.ppermute(value, axis, [(source, source + steps) for source in range(i...  153 us
    all_gather x1, waiting for transfers between devices, on_device(): whole_probe = jnp.sum(lax.all_gather(flat_probe, 'tr'), axis=0)  121 us
  transfers between devices with their start and end apart: 3, of which 2 were waited for; matrix products, arithmetic and copies ran while one was open for 5% of the time, Pallas kernels for 0%

profile of v1, /device:TPU:0, one launch (start us, length us, event | category | flops | bytes accessed | tf_op | source)
XLA Modules:
  0.0 349.8 jit_solution(16201542866637692058)
XLA Ops:
  7.2 0.0 copy-start.1
  7.2 0.0 all-gather.2.cloned.1.call-start
  7.2 3.2 slice.59
  10.5 1.3 collective-permute-start
  11.7 0.0 copy-done.1
  11.8 0.1 copy.19
  11.8 2.9 copy.18
  14.8 0.0 copy-start
  14.8 1.0 fusion.37
  15.8 1.1 negate_convert_fusion
  16.9 3.5 sqrt_bitcast_fusion
  20.4 0.0 collective-permute-done
  20.4 0.0 copy-done
  20.4 5.1 %pad_maximum_fusion = f32[2,768,1024]{2,1,0:T(8,128)} fusion(f32[2,256,1024]{2,1,0:T(8,128)} %collective-permute-done, f32[2,512,1024]{2,1,0:T(8,128)S(1)} %copy-done), kind=kLoop, calls=%fused_computation.53 | loop fusion | flops 1572864 | bytes 12582912 | tf_op jit(solution)/shard_map/concatenate | solution.py:89
  25.5 0.0 copy-start.2
  25.5 0.1 broadcast_in_dim.10
  25.6 3.4 broadcast_in_dim.4
  29.0 0.0 copy-done.2
  29.0 19.4 %while.12 = (s32[]{:T(128)}, f32[2,768,1024]{2,1,0:T(8,128)}, f32[2,2,256,256]{3,2,0,1:T(8,128)S(1)}, s32[]{:T(128)}, s32[8,2]{0,1:T(2,128)S(1)}, /*index=5*/f32...) while((s32[]{:T(128)}, f32[2,768,1024]{2,1,0:T(8,128)}, ...), condition=%wide.region_4.5_spmd, body=%wide.region_0.4_spmd.sunk | while | flops 1082195968 | bytes 27525448 | solution.py:109
  29.7 0.1 constant_dynamic-slice_fusion.3
  29.8 0.6 fusion.63
  34.4 1.3 dynamic-slice_bitcast_fusion.3
  35.7 0.2 fusion.64
  35.9 0.4 convolution_convert_fusion.3
  36.4 0.5 convolution_bitcast_fusion.2
  36.8 0.1 fusion.66
  36.9 1.0 fusion.67
  37.9 0.2 mul.321
  38.2 0.5 fusion.68
  38.7 0.5 fusion.70
  39.2 0.3 add_bitcast_fusion.2
  39.5 1.4 maximum_add_fusion.4
  40.8 0.3 maximum_add_fusion.5
  41.1 6.7 %dynamic_update_slice.4 = f32[2,768,1024]{2,1,0:T(8,128)} dynamic-update-slice(f32[2,768,1024]{2,1,0:T(8,128)} %get-tuple-element.216, f32[2,256,256]{2,1,0:T(8,128)S(1)} %maximum_add_fusion.4, s32[]{:T(128)} %constant.13.clone.1..sunk, s32[]{:T(128)S(6)} %select_n.47, s32[]{:T(128)S(6)} %select_n.48) | dynamic-update-slice | bytes 1048580 | tf_op jit(solution)/shard_map/while/body/dynamic_update_slice | solution.py:81
  48.5 1.1 copy.20
  49.5 0.0 all-gather.2.cloned.1.call-update
  49.6 3.2 slice.61
  52.7 152.1 %collective-permute-start.1 = (f32[2,256,1024]{2,1,0:T(8,128)}, f32[2,256,1024]{2,1,0:T(8,128)S(1)}, u32[]{:S(2)}, u32[]{:S(2)}) collective-permute-start(f32[2,256,1024]{2,1,0:T(8,128)} %slice.61), channel_id=1, source_target_pairs={{0,1},{1,2},{2,3},{3,4},{4,5},{5,6},{6,7},{7,8},{8,9},{9,10},{10,1... | collective-permute-start | bytes 6291464 | tf_op jit(solution)/shard_map/ppermute | solution.py:12
  204.9 3.8 %collective-permute-done.1 = f32[2,256,1024]{2,1,0:T(8,128)S(1)} collective-permute-done((f32[2,256,1024]{2,1,0:T(8,128)}, f32[2,256,1024]{2,1,0:T(8,128)S(1)}, u32[]{:S(2)}, u32[]{:S(2)}) %collective-permute-start.1) | collective-permute-done | bytes 2097184 | tf_op jit(solution)/shard_map/ppermute | solution.py:12
  208.7 5.6 %pad_add_fusion = f32[2,512,1024]{2,1,0:T(8,128)} fusion(f32[2,256,1024]{2,1,0:T(8,128)S(1)} %collective-permute-done.1, f32[2,768,1024]{2,1,0:T(8,128)} %get-tuple-element.51), kind=kLoop, calls=%fused_computation.54 | loop fusion | flops 1048576 | bytes 10485760 | tf_op jit(solution)/shard_map/add | solution.py:113
  214.3 121.0 %all-gather.2.cloned.1.call-done = f32[16,1024,256]{2,1,0:T(8,128)} async-done(((f32[1,1024,256]{2,1,0:T(8,128)}), f32[16,1024,256]{2,1,0:T(8,128)}) %all-gather.2.cloned.1.call-update) | async-done | bytes 16777232 | tf_op jit(solution)/shard_map/all_gather | solution.py:117
  335.3 7.0 %reduce_sum.36 = f32[1024,256]{1,0:T(8,128)S(1)} reduce(f32[16,1024,256]{2,1,0:T(8,128)} %all-gather.2.cloned.1.call-done, f32[]{:T(128)} %constant.22.clone.1), dimensions={0}, to_apply=%region_5.6 | reduce | flops 3932160 | bytes 17825796 | tf_op jit(solution)/shard_map/reduce_sum | solution.py:117
  342.3 0.6 constant_dynamic-slice_fusion.1
  (4 shorter events, 0.1 us)
Async XLA Ops:
  7.2 4.6 %copy-start.1 = (f32[2,2,256,256]{3,2,1,0:T(8,128)S(1)}, f32[2,2,256,256]{3,2,1,0:T(8,128)}, u32[]{:S(2)}) copy-start(f32[2,2,256,256]{3,2,1,0:T(8,128)} %param.8) | copy-start | bytes 3145732
  7.2 328.1 %all-gather.2.cloned.1.call-start = ((), (), s32[]{:S(2)}) async-start(), calls=%async_computation | async-start | bytes 17825792 | tf_op jit(solution)/shard_map/all_gather | solution.py:117
  10.5 9.9 %collective-permute-start = (f32[2,256,1024]{2,1,0:T(8,128)}, f32[2,256,1024]{2,1,0:T(8,128)}, u32[]{:S(2)}, u32[]{:S(2)}) collective-permute-start(f32[2,256,1024]{2,1,0:T(8,128)} %slice.59), channel_id=1, source_target_pairs={{1,0},{2,1},{3,2},{4,3},{5,4},{6,5},{7,6},{8,7},{9,8},{10,9},{11,1... | collective-permute-start | bytes 6291464 | tf_op jit(solution)/shard_map/ppermute | solution.py:12
  14.8 5.6 %copy-start = (f32[2,512,1024]{2,1,0:T(8,128)S(1)}, f32[2,512,1024]{2,1,0:T(8,128)}, u32[]{:S(2)}) copy-start(f32[2,512,1024]{2,1,0:T(8,128)} %param.7) | copy-start | bytes 12582916
  25.5 3.5 %copy-start.2 = (s32[1,8,2]{1,2,0:T(2,128)S(1)}, s32[1,8,2]{1,2,0:T(2,128)}, u32[]{:S(2)}) copy-start(s32[1,8,2]{1,2,0:T(2,128)} %param.9) | copy-start | bytes 196
  52.7 156.0 %collective-permute-start.1 = (f32[2,256,1024]{2,1,0:T(8,128)}, f32[2,256,1024]{2,1,0:T(8,128)S(1)}, u32[]{:S(2)}, u32[]{:S(2)}) collective-permute-start(f32[2,256,1024]{2,1,0:T(8,128)} %slice.61), channel_id=1, source_target_pairs={{0,1},{1,2},{2,3},{3,4},{4,5},{5,6},{6,7},{7,8},{8,9},{9,10},{10,1... | collective-permute-start | bytes 6291464 | tf_op jit(solution)/shard_map/ppermute | solution.py:12
Sparse Core Ops, SparseCore 0:
  49.7 285.5 all-gather.1
